TPU v7x, 128 devices: a whole 4x4x4 slice. The times are simulated.
128 devices in a mesh: gx: 16 (over x_hi, y, core), gy: 8 (over x_lo, z).
Axes of the slice: x: 4 (x_hi: 2, x_lo: 2; x = x_hi * 2 + x_lo), y: 4, z: 4, core: 2. Of those that a mesh axis runs over, the one named last changes fastest.
Arguments:
- values: bfloat16 [128, 32, 6, 128, 128], P('gx', 'gy'), may hold values from 0.019897461 to 1
- columns: int32 [128, 32, 6], P('gx', 'gy'), may hold values from 0 to 4095, as said below
- panel: float32 [128, 32, 128, 128], P('gx', 'gy'), as said below
Outputs:
- first_embedding: float32 [128, 32, 128, 128], P('gx', 'gy')
- embedding: float32 [128, 32, 128, 128], P('gx', 'gy')
- ritz: float32 [128, 128], replicated
Inputs may be any that keep to these rules, and one draw needn't show every extreme that they name: Each block column lies within one block of its block row along both grid directions: |columns // 32 - p| <= 1 and |columns % 32 - q| <= 1. `panel`: finite entries.
All inputs are finite; a program needn't handle non-finite values.
Results may differ from a plain program's by a relative error of at most 0.0003.
The roundings to bfloat16 on the way count: a program that leaves them out, or rounds other values in their place, can miss the bound.
Values may be sent and summed in bfloat16 or wider, within the bound.
A program may use at most 64 MiB of HBM per device.

v0:
```python
import jax
import jax.numpy as jnp
from jax import lax
from jax.sharding import PartitionSpec as P


def padded_2(cells, sides, width):
    for axis, dim in sides:
        count = lax.axis_size(axis)
        ends = count - 1
        head = lax.slice_in_dim(cells, 0, width, axis=dim)
        tail = lax.slice_in_dim(cells, cells.shape[dim] - width, cells.shape[dim], axis=dim)
        cells = jnp.concatenate(
            [
                lax.ppermute(tail, axis, [(i, (i + 1) % count) for i in range(ends)]),
                cells,
                lax.ppermute(head, axis, [((i + 1) % count, i) for i in range(ends)]),
            ],
            axis=dim,
        )
    return cells


def lower_inverse(gram):
    factor = jnp.linalg.cholesky(gram)
    width = gram.shape[0]
    ident = jnp.eye(width, dtype=jnp.float32)
    return lax.linalg.triangular_solve(factor, ident, left_side=True, lower=True)


def on_device(values, columns, panel):
    bx_dev, by_dev, blk, width = panel.shape
    nby_all = by_dev * lax.axis_size("gy")
    rows_all = bx_dev * by_dev * blk * lax.axis_size("gx") * lax.axis_size("gy")
    degree = jnp.sum(values, axis=(2, 4), dtype=jnp.float32)
    scale = 1.0 / jnp.sqrt(degree)
    local_x = columns // nby_all - lax.axis_index("gx") * bx_dev + 1
    local_y = columns % nby_all - lax.axis_index("gy") * by_dev + 1
    flat_index = local_x * (by_dev + 2) + local_y

    def apply_rows(scaled):
        padded = padded_2(scaled, (("gx", 0), ("gy", 1)), 1)
        table = padded.reshape(-1, blk, width)
        picked = table[flat_index]
        product = jnp.einsum(
            "abkij,abkjc->abic", values, picked, preferred_element_type=jnp.float32
        )
        return scale[..., None] * product

    def local_pair(left, right):
        return jnp.dot(
            left.reshape(-1, width).T, right.reshape(-1, width), precision=lax.Precision.HIGHEST
        )

    def normalize(iterate, inverse):
        flat = jnp.dot(iterate.reshape(-1, width), inverse.T, precision=lax.Precision.HIGHEST)
        return flat.reshape(iterate.shape)

    scaled = (scale[..., None] * panel).astype(jnp.bfloat16)
    first_iterate = apply_rows(scaled)
    first_gram = lax.psum(local_pair(first_iterate, first_iterate), ("gx", "gy")) / rows_all
    first_inverse = lower_inverse(first_gram)
    current = normalize(first_iterate, first_inverse)
    scaled = (scale[..., None] * current).astype(jnp.bfloat16)
    iterate = apply_rows(scaled)
    gram_sum = lax.psum(local_pair(iterate, iterate), ("gx", "gy"))
    inverse = lower_inverse(gram_sum / rows_all)
    image = apply_rows((scale[..., None] * iterate).astype(jnp.bfloat16))
    moment = lax.psum(local_pair(iterate, image), ("gx", "gy")) / rows_all
    embedding = normalize(iterate, inverse)
    ritz = jnp.dot(
        jnp.dot(inverse, moment, precision=lax.Precision.HIGHEST),
        inverse.T,
        precision=lax.Precision.HIGHEST,
    )
    return (current, embedding, ritz)


def solution(mesh):
    in_specs = (P("gx", "gy", None, None, None), P("gx", "gy", None), P("gx", "gy", None, None))
    out_specs = (P("gx", "gy", None, None), P("gx", "gy", None, None), P())
    return jax.shard_map(
        on_device, mesh=mesh, in_specs=in_specs, out_specs=out_specs, check_vma=False
    )
```

profile of v0, /device:TPU:1, one launch (start us, length us, event | category | flops | bytes accessed | tf_op | source)
XLA Modules:
  0.0 497.9 jit_solution(18421214030219309180)
XLA Ops:
  7.2 3.8 convert_reduce_fusion
  14.8 4.6 collective-permute-start
  21.3 4.3 collective-permute-done.1
  25.8 3.6 collective-permute-start.2
  39.9 8.1 %gather_fusion = bf16[192,128,128]{1,2,0:T(8,128)(2,1)} fusion(bf16[60,128,128]{1,2,0:T(8,128)(2,1)S(1)} %bitcast.118, s32[1024]{0:T(1024)S(1)} %pad_clamp_fusion), kind=kCustom, calls=%fused_computation | custom fusion | bytes 12583680 | tf_op jit(solution)/shard_map/gather | solution.py:44
  47.9 6.4 %fusion.53 = f32[8,4,128,128,1]{3,2,4,1,0:T(8,128)S(1)} fusion(bf16[8,4,6,128,128]{3,4,2,1,0:T(8,128)(2,1)} %bitcast.116, bf16[8,4,6,128,128]{4,3,2,1,0:T(8,128)(2,1)} %param.6), kind=kOutput, calls=%fused_computation.88 | convolution fusion | flops 805306368 | bytes 14680064 | tf_op jit(solution)/shard_map/abkij,abkjc->abic/dot_general | solution.py:45
  57.0 143.5 %all-reduce.4.cloned.1.call-done = f32[128,128]{0,1:T(8,128)} async-done(((f32[128,128]{0,1:T(8,128)}), f32[128,128]{0,1:T(8,128)}) %all-reduce.4.cloned.1.call-update) | async-done | bytes 65552 | tf_op jit(solution)/shard_map/psum | solution.py:61
  202.3 11.7 %cholesky.44 = f32[128,128]{1,0:T(8,128)S(1)} custom-call(f32[128,128]{1,0:T(8,128)S(1)} %fusion.37), custom_call_target="Cholesky" | custom-call | tf_op jit(solution)/shard_map/jit(cholesky)/cholesky | solution.py:25
  215.4 9.8 %custom-call.6 = f32[1,128,128]{1,2,0:T(8,128)S(1)} custom-call(f32[1,128,128]{2,1,0:T(8,128)S(1)} %fusion.31), custom_call_target="InvertDiagBlocksLowerTriangular" | custom-call | tf_op jit(solution)/shard_map/triangular_solve/custom-call.0 | solution.py:28
  225.5 4.8 fusion.8
  236.8 4.2 collective-permute-done.5
  245.3 3.9 collective-permute-done.6
  249.2 4.1 collective-permute-done.7
  253.7 8.1 %gather_fusion.1 = bf16[192,128,128]{1,2,0:T(8,128)(2,1)} fusion(bf16[60,128,128]{1,2,0:T(8,128)(2,1)S(1)} %bitcast.119, s32[1024]{0:T(1024)S(1)} %pad_clamp_fusion), kind=kCustom, calls=%fused_computation.1 | custom fusion | bytes 12583680 | tf_op jit(solution)/shard_map/gather | solution.py:44
  261.7 6.4 %fusion.7 = (bf16[8,4,128,128]{2,3,1,0:T(8,128)(2,1)S(1)}, f32[8,4,128,128,1]{3,2,4,1,0:T(8,128)S(1)}) fusion(f32[8,4,128]{2,1,0:T(4,128)S(1)} %sqrt.3, bf16[8,4,6,128,128]{3,4,2,1,0:T(8,128)(2,1)} %bitcast.114, bf16[8,4,6,128,128]{4,3,2,1,0:T(8,128)(2,1)} %param.6), kind=kOutput, calls=%fused_computation.13 | convolution fusion | flops 806879232 | bytes 15745024 | tf_op jit(solution)/shard_map/abkij,abkjc->abic/dot_general | solution.py:45
  268.2 5.0 collective-permute-start.8
  275.1 4.3 collective-permute-done.9
  286.7 4.1 collective-permute-done.11
  292.4 9.8 %gather_fusion.2 = bf16[192,128,128]{1,2,0:T(8,128)(2,1)} fusion(bf16[60,128,128]{1,2,0:T(8,128)(2,1)} %bitcast.117, s32[1024]{0:T(1024)S(1)} %pad_clamp_fusion), kind=kCustom, calls=%fused_computation.2 | custom fusion | bytes 12583680 | tf_op jit(solution)/shard_map/gather | solution.py:44
  302.2 6.4 %fusion.54 = f32[8,4,128,128,1]{3,2,4,1,0:T(8,128)S(1)} fusion(bf16[8,4,6,128,128]{3,4,2,1,0:T(8,128)(2,1)} %bitcast.115, bf16[8,4,6,128,128]{4,3,2,1,0:T(8,128)(2,1)} %param.6), kind=kOutput, calls=%fused_computation.89 | convolution fusion | flops 805306368 | bytes 14680064 | tf_op jit(solution)/shard_map/abkij,abkjc->abic/dot_general | solution.py:45
  311.3 148.5 %all-reduce.6.cloned.1.call-done = (f32[128,128]{0,1:T(8,128)}, f32[128,128]{0,1:T(8,128)}) async-done(((f32[128,128]{0,1:T(8,128)}, f32[128,128]{0,1:T(8,128)}), (f32[128,128]{0,1:T(8,128)}, f32[128,128]{0,1:T(8,128)})) %all-reduce.6.cloned.1.call-update) | async-done | bytes 131088 | tf_op jit(solution)/shard_map/psum | solution.py:66
  461.6 11.7 %cholesky.55 = f32[128,128]{1,0:T(8,128)S(1)} custom-call(f32[128,128]{1,0:T(8,128)S(1)} %fusion.35), custom_call_target="Cholesky" | custom-call | tf_op jit(solution)/shard_map/jit(cholesky)/cholesky | solution.py:25
  474.6 9.8 %custom-call.7 = f32[1,128,128]{1,2,0:T(8,128)S(1)} custom-call(f32[1,128,128]{2,1,0:T(8,128)S(1)} %fusion.32), custom_call_target="InvertDiagBlocksLowerTriangular" | custom-call | tf_op jit(solution)/shard_map/triangular_solve/custom-call.0 | solution.py:28
  484.7 4.8 fusion.3
  (64 shorter events, 51.5 us)
Async XLA Ops:
  7.2 3.9 copy-start
  7.2 193.3 %all-reduce.4.cloned.1.call-start = ((), (), s32[]{:S(2)}) async-start(), calls=%async_computation | async-start | bytes 131072 | tf_op jit(solution)/shard_map/psum | solution.py:61
  12.9 17.7 %copy-start.3 = (s32[8,4,6]{0,1,2:T(4,128)S(1)}, s32[8,4,6]{0,1,2:T(4,128)}, u32[]{:S(2)}) copy-start(s32[8,4,6]{0,1,2:T(4,128)} %param.7) | copy-start | bytes 2308
  14.8 6.5 %collective-permute-start = (bf16[1,4,128,128]{2,3,1,0:T(8,128)(2,1)S(1)}, bf16[1,4,128,128]{2,3,1,0:T(8,128)(2,1)S(1)}, u32[]{:S(2)}, u32[]{:S(2)}) collective-permute-start(bf16[1,4,128,128]{2,3,1,0:T(8,128)(2,1)S(1)} %get-tuple-element.17), channel_id=1, source_target_pairs={{0,8},{8,16},{16,24},{24,32},{32,40},{40,48},{48,56},{56,64},{64,7... | collective-permute-start | bytes 393224 | tf_op jit(solution)/shard_map/ppermute | solution.py:15
  19.4 6.3 %collective-permute-start.1 = (bf16[1,4,128,128]{2,3,1,0:T(8,128)(2,1)S(1)}, bf16[1,4,128,128]{2,3,1,0:T(8,128)(2,1)S(1)}, u32[]{:S(2)}, u32[]{:S(2)}) collective-permute-start(bf16[1,4,128,128]{2,3,1,0:T(8,128)(2,1)S(1)} %get-tuple-element.18), channel_id=1, source_target_pairs={{8,0},{16,8},{24,16},{32,24},{40,32},{48,40},{56,48},{64,56},{72,6... | collective-permute-start | bytes 393224 | tf_op jit(solution)/shard_map/ppermute | solution.py:17
  25.8 8.5 %collective-permute-start.2 = (bf16[10,1,128,128]{2,3,1,0:T(8,128)(2,1)S(1)}, bf16[10,1,128,128]{2,3,1,0:T(8,128)(2,1)S(1)}, u32[]{:S(2)}, u32[]{:S(2)}) collective-permute-start(bf16[10,1,128,128]{2,3,1,0:T(8,128)(2,1)S(1)} %get-tuple-element.11), channel_id=1, source_target_pairs={{0,1},{1,2},{2,3},{3,4},{4,5},{5,6},{6,7},{8,9},{9,10},{10,11},{11... | collective-permute-start | bytes 983048 | tf_op jit(solution)/shard_map/ppermute | solution.py:15
  29.3 9.1 %collective-permute-start.3 = (bf16[10,1,128,128]{2,3,1,0:T(8,128)(2,1)S(1)}, bf16[10,1,128,128]{2,3,1,0:T(8,128)(2,1)}, u32[]{:S(2)}, u32[]{:S(2)}) collective-permute-start(bf16[10,1,128,128]{2,3,1,0:T(8,128)(2,1)S(1)} %get-tuple-element.12), channel_id=1, source_target_pairs={{1,0},{2,1},{3,2},{4,3},{5,4},{6,5},{7,6},{9,8},{10,9},{11,10},{12... | collective-permute-start | bytes 983048 | tf_op jit(solution)/shard_map/ppermute | solution.py:17
  34.3 0.7 copy-start.1
  56.8 403.0 %all-reduce.6.cloned.1.call-start = ((), (), s32[]{:S(2)}) async-start(), calls=%async_computation.1 | async-start | bytes 262144 | tf_op jit(solution)/shard_map/psum | solution.py:66
  232.4 4.3 collective-permute-start.4
  234.7 6.3 %collective-permute-start.5 = (bf16[1,4,128,128]{2,3,1,0:T(8,128)(2,1)S(1)}, bf16[1,4,128,128]{2,3,1,0:T(8,128)(2,1)S(1)}, u32[]{:S(2)}, u32[]{:S(2)}) collective-permute-start(bf16[1,4,128,128]{2,3,1,0:T(8,128)(2,1)S(1)} %get-tuple-element.16), channel_id=1, source_target_pairs={{8,0},{16,8},{24,16},{32,24},{40,32},{48,40},{56,48},{64,56},{72,6... | collective-permute-start | bytes 393224 | tf_op jit(solution)/shard_map/ppermute | solution.py:17
  241.1 8.2 %collective-permute-start.6 = (bf16[10,1,128,128]{2,3,1,0:T(8,128)(2,1)S(1)}, bf16[10,1,128,128]{2,3,1,0:T(8,128)(2,1)S(1)}, u32[]{:S(2)}, u32[]{:S(2)}) collective-permute-start(bf16[10,1,128,128]{2,3,1,0:T(8,128)(2,1)S(1)} %get-tuple-element.9), channel_id=1, source_target_pairs={{0,1},{1,2},{2,3},{3,4},{4,5},{5,6},{6,7},{8,9},{9,10},{10,11},{11... | collective-permute-start | bytes 983048 | tf_op jit(solution)/shard_map/ppermute | solution.py:15
  243.8 9.5 %collective-permute-start.7 = (bf16[10,1,128,128]{2,3,1,0:T(8,128)(2,1)S(1)}, bf16[10,1,128,128]{2,3,1,0:T(8,128)(2,1)S(1)}, u32[]{:S(2)}, u32[]{:S(2)}) collective-permute-start(bf16[10,1,128,128]{2,3,1,0:T(8,128)(2,1)S(1)} %get-tuple-element.10), channel_id=1, source_target_pairs={{1,0},{2,1},{3,2},{4,3},{5,4},{6,5},{7,6},{9,8},{10,9},{11,10},{12... | collective-permute-start | bytes 983048 | tf_op jit(solution)/shard_map/ppermute | solution.py:17
  268.2 6.9 %collective-permute-start.8 = (bf16[1,4,128,128]{2,3,1,0:T(8,128)(2,1)S(1)}, bf16[1,4,128,128]{2,3,1,0:T(8,128)(2,1)S(1)}, u32[]{:S(2)}, u32[]{:S(2)}) collective-permute-start(bf16[1,4,128,128]{2,3,1,0:T(8,128)(2,1)S(1)} %get-tuple-element.13), channel_id=1, source_target_pairs={{0,8},{8,16},{16,24},{24,32},{32,40},{40,48},{48,56},{56,64},{64,7... | collective-permute-start | bytes 393224 | tf_op jit(solution)/shard_map/ppermute | solution.py:15
  273.1 6.3 %collective-permute-start.9 = (bf16[1,4,128,128]{2,3,1,0:T(8,128)(2,1)S(1)}, bf16[1,4,128,128]{2,3,1,0:T(8,128)(2,1)S(1)}, u32[]{:S(2)}, u32[]{:S(2)}) collective-permute-start(bf16[1,4,128,128]{2,3,1,0:T(8,128)(2,1)S(1)} %get-tuple-element.14), channel_id=1, source_target_pairs={{8,0},{16,8},{24,16},{32,24},{40,32},{48,40},{56,48},{64,56},{72,6... | collective-permute-start | bytes 393224 | tf_op jit(solution)/shard_map/ppermute | solution.py:17
  279.5 7.2 %collective-permute-start.10 = (bf16[10,1,128,128]{2,3,1,0:T(8,128)(2,1)S(1)}, bf16[10,1,128,128]{2,3,1,0:T(8,128)(2,1)S(1)}, u32[]{:S(2)}, u32[]{:S(2)}) collective-permute-start(bf16[10,1,128,128]{2,3,1,0:T(8,128)(2,1)S(1)} %get-tuple-element.7), channel_id=1, source_target_pairs={{0,1},{1,2},{2,3},{3,4},{4,5},{5,6},{6,7},{8,9},{9,10},{10,11},{11... | collective-permute-start | bytes 983048 | tf_op jit(solution)/shard_map/ppermute | solution.py:15
  281.8 9.0 %collective-permute-start.11 = (bf16[10,1,128,128]{2,3,1,0:T(8,128)(2,1)S(1)}, bf16[10,1,128,128]{2,3,1,0:T(8,128)(2,1)S(1)}, u32[]{:S(2)}, u32[]{:S(2)}) collective-permute-start(bf16[10,1,128,128]{2,3,1,0:T(8,128)(2,1)S(1)} %get-tuple-element.8), channel_id=1, source_target_pairs={{1,0},{2,1},{3,2},{4,3},{5,4},{6,5},{7,6},{9,8},{10,9},{11,10},{12... | collective-permute-start | bytes 983048 | tf_op jit(solution)/shard_map/ppermute | solution.py:17
  484.7 4.8 copy-start.2
Sparse Core Ops, SparseCore 0:
  56.9 143.5 all-reduce.3
  311.4 148.3 all-reduce.5
where the time goes:
time: 505 us; the launch traced here: 498 us
  waiting for transfers between devices  325 us (64%)
  other arithmetic  58.6 us (12%)
  matrix products  38 us (8%)
  local copies, waits for them, and re-layouts  30.9 us (6%)
  starting transfers between devices  30.6 us (6%)
  between operations  14.8 us (3%)
    psum x1, waiting for transfers between devices, on_device(): gram_sum = lax.psum(local_pair(iterate, iterate), ('gx', 'gy'))  148 us
    psum x1, waiting for transfers between devices, on_device(): lax.psum(local_pair(first_iterate, first_iterate), ('gx', 'gy')) / rows_all  143 us
    gather x3, local copies, waits for them, and re-layouts, apply_rows(): picked = table[flat_index]  26 us
    another operation x6, other arithmetic, lower_inverse(): factor = jnp.linalg.cholesky(gram)  24.8 us
    ppermute x6, waiting for transfers between devices, padded_2(): lax.ppermute(head, axis, [((i + 1) % count, i) for i in range(ends)])  24.6 us
    another operation x4, other arithmetic, lower_inverse(): lax.linalg.triangular_solve(factor, ident, left_side=True, lower=True)  20.9 us
    ppermute x6, starting transfers between devices, padded_2(): lax.ppermute(tail, axis, [(i, (i + 1) % count) for i in range(ends)])  20.3 us
    dot_general x3, matrix products, apply_rows(): jnp.einsum('abkij,abkjc->abic', values, picked, preferred_element_type=jn...  19.2 us
  transfers between devices with their start and end apart: 14, of which 11 were waited for; matrix products, arithmetic and copies ran while one was open for 1% of the time, Pallas kernels for 0%

commit v1 on v0

--- a/solution.py
+++ b/solution.py
@@ -1,9 +1,107 @@
+import functools
+
 import jax
 import jax.numpy as jnp
 from jax import lax
+from jax.experimental import pallas as pl
+from jax.experimental.pallas import tpu as pltpu
 from jax.sharding import PartitionSpec as P
 
+NEAR = 8
+FAR = 16
+STRIP = 16
 
+
+def near_partner(step):
+    gx = lax.axis_index("gx")
+    base = (gx // NEAR) * NEAR
+    at = lax.rem(gx - base + step, NEAR)
+    return at, (base + at, lax.axis_index("gy"))
+
+
+def far_partner(step):
+    gx, gy = lax.axis_index("gx"), lax.axis_index("gy")
+    place = (gx // NEAR) * 8 + gy
+    to = lax.rem(place + step, FAR)
+    return to, ((to // 8) * NEAR + lax.rem(gx, NEAR), lax.rem(to, 8))
+
+
+def remote(src, dst, send, recv, device):
+    return pltpu.make_async_remote_copy(
+        src_ref=src, dst_ref=dst, send_sem=send, recv_sem=recv,
+        device_id=device, device_id_type=pl.DeviceIdType.MESH,
+    )
+
+
+def strip_of(ref, at):
+    return ref.at[pl.ds(pl.multiple_of(at * STRIP, STRIP), STRIP)]
+
+
+def sum_kernel(mine, out, near_buf, mid, far_buf, done, s1, r1, s2, r2, s3, r3):
+    barrier = pltpu.get_barrier_semaphore()
+    for step in range(1, NEAR):
+        pl.semaphore_signal(barrier, inc=1, device_id=near_partner(step)[1], device_id_type=pl.DeviceIdType.MESH)
+    for step in range(1, FAR):
+        pl.semaphore_signal(barrier, inc=1, device_id=far_partner(step)[1], device_id_type=pl.DeviceIdType.MESH)
+    pl.semaphore_wait(barrier, NEAR + FAR - 2)
+    gx, gy = lax.axis_index("gx"), lax.axis_index("gy")
+    near = lax.rem(gx, NEAR)
+    far = (gx // NEAR) * 8 + gy
+
+    first = []
+    for step in range(1, NEAR):
+        at, device = near_partner(step)
+        copy = remote(strip_of(mine, at), near_buf.at[near], s1.at[step], r1.at[step], device)
+        copy.start()
+        first.append(copy)
+    near_buf[near] = strip_of(mine, near)[...]
+    for copy in first:
+        copy.wait()
+    part = near_buf[0]
+    for i in range(1, NEAR):
+        part = part + near_buf[i]
+    mid[...] = part
+    far_buf[far] = part
+    second = []
+    for step in range(1, FAR):
+        _, device = far_partner(step)
+        copy = remote(mid, far_buf.at[far], s2.at[step], r2.at[step], device)
+        copy.start()
+        second.append(copy)
+    for copy in second:
+        copy.wait()
+    part = far_buf[0]
+    for i in range(1, FAR):
+        part = part + far_buf[i]
+    done[...] = part
+    strip_of(out, near)[...] = part
+    third = []
+    for step in range(1, NEAR):
+        _, device = near_partner(step)
+        copy = remote(done, strip_of(out, near), s3.at[step], r3.at[step], device)
+        copy.start()
+        third.append(copy)
+    for copy in third:
+        copy.wait()
+
+
+def sum_all(mine, ident):
+    dma = pltpu.SemaphoreType.DMA
+    return pl.pallas_call(
+        sum_kernel,
+        out_shape=jax.ShapeDtypeStruct(mine.shape, jnp.float32),
+        in_specs=[pl.BlockSpec(memory_space=pltpu.VMEM)],
+        out_specs=pl.BlockSpec(memory_space=pltpu.VMEM),
+        scratch_shapes=[
+            pltpu.VMEM((NEAR, STRIP, 128), jnp.float32),
+            pltpu.VMEM((STRIP, 128), jnp.float32),
+            pltpu.VMEM((FAR, STRIP, 128), jnp.float32),
+            pltpu.VMEM((STRIP, 128), jnp.float32),
+            dma((NEAR,)), dma((NEAR,)), dma((FAR,)), dma((FAR,)), dma((NEAR,)), dma((NEAR,)),
+        ],
+        compiler_params=pltpu.CompilerParams(collective_id=ident, has_side_effects=True),
+        name="sum_all_%d" % ident,
+    )(mine)
 def padded_2(cells, sides, width):
     for axis, dim in sides:
         count = lax.axis_size(axis)
@@ -58,15 +156,15 @@
 
     scaled = (scale[..., None] * panel).astype(jnp.bfloat16)
     first_iterate = apply_rows(scaled)
-    first_gram = lax.psum(local_pair(first_iterate, first_iterate), ("gx", "gy")) / rows_all
+    first_gram = sum_all(local_pair(first_iterate, first_iterate), 0) / rows_all
     first_inverse = lower_inverse(first_gram)
     current = normalize(first_iterate, first_inverse)
     scaled = (scale[..., None] * current).astype(jnp.bfloat16)
     iterate = apply_rows(scaled)
-    gram_sum = lax.psum(local_pair(iterate, iterate), ("gx", "gy"))
+    gram_sum = sum_all(local_pair(iterate, iterate), 1)
     inverse = lower_inverse(gram_sum / rows_all)
     image = apply_rows((scale[..., None] * iterate).astype(jnp.bfloat16))
-    moment = lax.psum(local_pair(iterate, image), ("gx", "gy")) / rows_all
+    moment = sum_all(local_pair(iterate, image), 2) / rows_all
     embedding = normalize(iterate, inverse)
     ritz = jnp.dot(
         jnp.dot(inverse, moment, precision=lax.Precision.HIGHEST),

time: 505 us -> 271 us (0.54)
  waiting for transfers between devices: 325 us -> 27.5 us
  Pallas kernels: 0 us -> 70 us
  between operations: 14.8 us -> 1.24 us
    psum x2 -> x0, waiting for transfers between devices: 292 us -> none  [the longest x1 148 us: on_device(): gram_sum = lax.psum(local_pair(iterate, iterate), ('gx', 'gy'))]
    pallas_call x0 -> x3, Pallas kernels: none -> 70 us  [sum_all(): pl.pallas_call(sum_kernel, out_shape=jax.ShapeDtypeStruct(mine.shape, jnp...]
  transfers between devices with their start and end apart: 14 -> 12, of which waited for: 11 -> 8; matrix products, arithmetic and copies ran while one was open for 1% -> 15% of each run, Pallas kernels for 0% -> 10%
where the time goes in v1:
time: 271 us; the launch traced here: 266 us
  Pallas kernels  70 us (26%)
  other arithmetic  62.9 us (23%)
  matrix products  40 us (15%)
  local copies, waits for them, and re-layouts  34.1 us (13%)
  starting transfers between devices  29.7 us (11%)
  waiting for transfers between devices  27.5 us (10%)
    pallas_call x3, Pallas kernels, sum_all(): pl.pallas_call(sum_kernel, out_shape=jax.ShapeDtypeStruct(mine.shape, jnp...  70 us
    gather x3, local copies, waits for them, and re-layouts, apply_rows(): picked = table[flat_index]  26 us
    another operation x6, other arithmetic, lower_inverse(): factor = jnp.linalg.cholesky(gram)  25.7 us
    another operation x4, other arithmetic, lower_inverse(): lax.linalg.triangular_solve(factor, ident, left_side=True, lower=True)  23 us
    ppermute x6, waiting for transfers between devices, padded_2(): lax.ppermute(head, axis, [((i + 1) % count, i) for i in range(ends)])  19.9 us
    ppermute x6, starting transfers between devices, padded_2(): lax.ppermute(tail, axis, [(i, (i + 1) % count) for i in range(ends)])  19.5 us
    dot_general x3, matrix products, apply_rows(): jnp.einsum('abkij,abkjc->abic', values, picked, preferred_element_type=jn...  19.2 us
    ppermute x6, starting transfers between devices, padded_2(): lax.ppermute(head, axis, [((i + 1) % count, i) for i in range(ends)])  10.3 us
  transfers between devices with their start and end apart: 12, of which 8 were waited for; matrix products, arithmetic and copies ran while one was open for 15% of the time, Pallas kernels for 10%

profile of v1, /device:TPU:1, one launch (start us, length us, event | category | flops | bytes accessed | tf_op | source)
XLA Modules:
  0.0 265.5 jit_solution(9501244677016956979)
XLA Ops:
  0.6 3.8 %convert_reduce_fusion = f32[8,4,128]{2,1,0:T(4,128)S(1)} fusion(bf16[8,4,6,128,128]{4,3,2,1,0:T(8,128)(2,1)} %param.6), kind=kLoop, calls=%fused_computation.3 | loop fusion | flops 6287360 | bytes 6307840 | tf_op jit(solution)/shard_map/reduce_sum | solution.py:133
  8.2 4.6 %collective-permute-start = (bf16[1,4,128,128]{2,3,1,0:T(8,128)(2,1)S(1)}, bf16[1,4,128,128]{2,3,1,0:T(8,128)(2,1)S(1)}, u32[]{:S(2)}, u32[]{:S(2)}) collective-permute-start(bf16[1,4,128,128]{2,3,1,0:T(8,128)(2,1)S(1)} %get-tuple-element.15), channel_id=1, source_target_pairs={{0,8},{8,16},{16,24},{24,32},{32,40},{40,48},{48,56},{56,64},{64,7... | collective-permute-start | bytes 393224 | tf_op jit(solution)/shard_map/ppermute | solution.py:113
  14.8 4.3 %collective-permute-done.1 = bf16[1,4,128,128]{2,3,1,0:T(8,128)(2,1)S(1)} collective-permute-done((bf16[1,4,128,128]{2,3,1,0:T(8,128)(2,1)S(1)}, bf16[1,4,128,128]{2,3,1,0:T(8,128)(2,1)S(1)}, u32[]{:S(2)}, u32[]{:S(2)}) %collective-permute-start.1) | collective-permute-done | bytes 131104 | tf_op jit(solution)/shard_map/ppermute | solution.py:115
  19.2 3.6 %collective-permute-start.2 = (bf16[10,1,128,128]{2,3,1,0:T(8,128)(2,1)S(1)}, bf16[10,1,128,128]{2,3,1,0:T(8,128)(2,1)S(1)}, u32[]{:S(2)}, u32[]{:S(2)}) collective-permute-start(bf16[10,1,128,128]{2,3,1,0:T(8,128)(2,1)S(1)} %get-tuple-element.9), channel_id=1, source_target_pairs={{0,1},{1,2},{2,3},{3,4},{4,5},{5,6},{6,7},{8,9},{9,10},{10,11},{11... | collective-permute-start | bytes 983048 | tf_op jit(solution)/shard_map/ppermute | solution.py:113
  33.3 8.3 %gather_fusion = bf16[192,128,128]{1,2,0:T(8,128)(2,1)} fusion(bf16[60,128,128]{1,2,0:T(8,128)(2,1)S(1)} %bitcast.122, s32[1024]{0:T(1024)S(1)} %pad_clamp_fusion), kind=kCustom, calls=%fused_computation | custom fusion | bytes 12583680 | tf_op jit(solution)/shard_map/gather | solution.py:142
  41.6 6.4 %fusion.53 = f32[8,4,128,128,1]{3,2,4,1,0:T(8,128)S(1)} fusion(bf16[8,4,6,128,128]{3,4,2,1,0:T(8,128)(2,1)} %bitcast.120, bf16[8,4,6,128,128]{4,3,2,1,0:T(8,128)(2,1)} %param.6), kind=kOutput, calls=%fused_computation.88 | convolution fusion | flops 805306368 | bytes 14680064 | tf_op jit(solution)/shard_map/abkij,abkjc->abic/dot_general | solution.py:143
  50.5 23.3 %sum_all_0.1 = f32[128,128]{1,0:T(8,128)} custom-call(f32[128,128]{1,0:T(8,128)} %fusion.12.mine), custom_call_target="tpu_custom_call" | custom-call | tf_op jit(solution)/shard_map/sum_all_0/pallas_call | solution.py:90
  75.7 11.7 %cholesky.44 = f32[128,128]{1,0:T(8,128)S(1)} custom-call(f32[128,128]{1,0:T(8,128)S(1)} %copy.20), custom_call_target="Cholesky" | custom-call | tf_op jit(solution)/shard_map/jit(cholesky)/cholesky | solution.py:123
  88.7 9.8 %custom-call.6 = f32[1,128,128]{1,2,0:T(8,128)S(1)} custom-call(f32[1,128,128]{2,1,0:T(8,128)S(1)} %fusion.31), custom_call_target="InvertDiagBlocksLowerTriangular" | custom-call | tf_op jit(solution)/shard_map/triangular_solve/custom-call.0 | solution.py:126
  98.8 5.3 %fusion.8 = f32[8,4,128,128]{3,2,1,0:T(8,128)} fusion(f32[128,128,1,1]{1,0,3,2:T(8,128)S(1)} %convolution_bitcast_fusion, f32[8,4,128,128,1]{3,2,4,1,0:T(8,128)S(1)} %fusion.53, f32[8,4,128]{2,1,0:T(4,128)S(1)} %sqrt.3), kind=kOutput, calls=%fused_computation.15 | convolution fusion | flops 805830656 | bytes 4276224 | tf_op jit(solution)/shard_map/dot_general | solution.py:154
  110.7 4.1 %collective-permute-done.5 = bf16[1,4,128,128]{2,3,1,0:T(8,128)(2,1)S(1)} collective-permute-done((bf16[1,4,128,128]{2,3,1,0:T(8,128)(2,1)S(1)}, bf16[1,4,128,128]{2,3,1,0:T(8,128)(2,1)S(1)}, u32[]{:S(2)}, u32[]{:S(2)}) %collective-permute-start.5) | collective-permute-done | bytes 131104 | tf_op jit(solution)/shard_map/ppermute | solution.py:115
  118.4 3.9 %collective-permute-done.6 = bf16[10,1,128,128]{2,3,1,0:T(8,128)(2,1)S(1)} collective-permute-done((bf16[10,1,128,128]{2,3,1,0:T(8,128)(2,1)S(1)}, bf16[10,1,128,128]{2,3,1,0:T(8,128)(2,1)S(1)}, u32[]{:S(2)}, u32[]{:S(2)}) %collective-permute-start.6) | collective-permute-done | bytes 327712 | tf_op jit(solution)/shard_map/ppermute | solution.py:113
  122.3 4.1 %collective-permute-done.7 = bf16[10,1,128,128]{2,3,1,0:T(8,128)(2,1)S(1)} collective-permute-done((bf16[10,1,128,128]{2,3,1,0:T(8,128)(2,1)S(1)}, bf16[10,1,128,128]{2,3,1,0:T(8,128)(2,1)S(1)}, u32[]{:S(2)}, u32[]{:S(2)}) %collective-permute-start.7) | collective-permute-done | bytes 327712 | tf_op jit(solution)/shard_map/ppermute | solution.py:115
  126.8 8.1 %gather_fusion.1 = bf16[192,128,128]{1,2,0:T(8,128)(2,1)} fusion(bf16[60,128,128]{1,2,0:T(8,128)(2,1)S(1)} %bitcast.123, s32[1024]{0:T(1024)S(1)} %pad_clamp_fusion), kind=kCustom, calls=%fused_computation.1 | custom fusion | bytes 12583680 | tf_op jit(solution)/shard_map/gather | solution.py:142
  134.8 6.4 %fusion.7 = (bf16[8,4,128,128]{2,3,1,0:T(8,128)(2,1)S(1)}, f32[8,4,128,128,1]{3,2,4,1,0:T(8,128)S(1)}) fusion(f32[8,4,128]{2,1,0:T(4,128)S(1)} %sqrt.3, bf16[8,4,6,128,128]{3,4,2,1,0:T(8,128)(2,1)} %bitcast.118, bf16[8,4,6,128,128]{4,3,2,1,0:T(8,128)(2,1)} %param.6), kind=kOutput, calls=%fused_computation.13 | convolution fusion | flops 806879232 | bytes 15745024 | tf_op jit(solution)/shard_map/abkij,abkjc->abic/dot_general | solution.py:143
  141.9 4.6 %collective-permute-start.8 = (bf16[1,4,128,128]{2,3,1,0:T(8,128)(2,1)}, bf16[1,4,128,128]{2,3,1,0:T(8,128)(2,1)S(1)}, u32[]{:S(2)}, u32[]{:S(2)}) collective-permute-start(bf16[1,4,128,128]{2,3,1,0:T(8,128)(2,1)} %get-tuple-element.11), channel_id=1, source_target_pairs={{0,8},{8,16},{16,24},{24,32},{32,40},{40,48},{48,56},{56,64},{64,7... | collective-permute-start | bytes 393224 | tf_op jit(solution)/shard_map/ppermute | solution.py:113
  151.1 25.2 %sum_all_1.1 = f32[128,128]{1,0:T(8,128)} custom-call(f32[128,128]{1,0:T(8,128)} %fusion.15.mine), custom_call_target="tpu_custom_call" | custom-call | tf_op jit(solution)/shard_map/sum_all_1/pallas_call | solution.py:90
  181.8 12.5 %cholesky.55 = f32[128,128]{1,0:T(8,128)S(1)} custom-call(f32[128,128]{1,0:T(8,128)} %copy.25), custom_call_target="Cholesky" | custom-call | tf_op jit(solution)/shard_map/jit(cholesky)/cholesky | solution.py:123
  196.3 11.3 %custom-call.7 = f32[1,128,128]{1,2,0:T(8,128)} custom-call(f32[1,128,128]{2,1,0:T(8,128)} %fusion.32), custom_call_target="InvertDiagBlocksLowerTriangular" | custom-call | tf_op jit(solution)/shard_map/triangular_solve/custom-call.0 | solution.py:126
  212.6 4.8 %fusion.3 = f32[8,4,128,128]{3,2,1,0:T(8,128)} fusion(f32[8,4,128,128,1]{3,2,4,1,0:T(8,128)S(1)} %get-tuple-element.18, f32[8,4,128]{2,1,0:T(4,128)S(1)} %sqrt.3, f32[128,128]{1,0:T(8,128)S(1)} %fusion.28), kind=kOutput, calls=%fused_computation.9 | convolution fusion | flops 805830656 | bytes 4276224 | tf_op jit(solution)/shard_map/dot_general | solution.py:154
  217.7 3.9 %collective-permute-done.11 = bf16[10,1,128,128]{2,3,1,0:T(8,128)(2,1)S(1)} collective-permute-done((bf16[10,1,128,128]{2,3,1,0:T(8,128)(2,1)S(1)}, bf16[10,1,128,128]{2,3,1,0:T(8,128)(2,1)S(1)}, u32[]{:S(2)}, u32[]{:S(2)}) %collective-permute-start.11) | collective-permute-done | bytes 327712 | tf_op jit(solution)/shard_map/ppermute | solution.py:115
  223.2 9.6 %gather_fusion.2 = bf16[192,128,128]{1,2,0:T(8,128)(2,1)} fusion(bf16[60,128,128]{1,2,0:T(8,128)(2,1)} %bitcast.121, s32[1024]{0:T(1024)S(1)} %pad_clamp_fusion), kind=kCustom, calls=%fused_computation.2 | custom fusion | bytes 12583680 | tf_op jit(solution)/shard_map/gather | solution.py:142
  232.8 6.4 %fusion.54 = f32[8,4,128,128,1]{3,2,4,1,0:T(8,128)S(1)} fusion(bf16[8,4,6,128,128]{3,4,2,1,0:T(8,128)(2,1)} %bitcast.119, bf16[8,4,6,128,128]{4,3,2,1,0:T(8,128)(2,1)} %param.6), kind=kOutput, calls=%fused_computation.89 | convolution fusion | flops 805306368 | bytes 14680064 | tf_op jit(solution)/shard_map/abkij,abkjc->abic/dot_general | solution.py:143
  241.8 21.5 %sum_all_2.1 = f32[128,128]{1,0:T(8,128)} custom-call(f32[128,128]{1,0:T(8,128)} %fusion.18.mine), custom_call_target="tpu_custom_call" | custom-call | tf_op jit(solution)/shard_map/sum_all_2/pallas_call | solution.py:90
  (61 shorter events, 56.8 us)
Async XLA Ops:
  0.6 3.9 %copy-start = (f32[8,4,128,128]{3,2,1,0:T(8,128)S(1)}, f32[8,4,128,128]{3,2,1,0:T(8,128)}, u32[]{:S(2)}) copy-start(f32[8,4,128,128]{3,2,1,0:T(8,128)} %param.8) | copy-start | bytes 6291460
  6.3 17.7 %copy-start.2 = (s32[8,4,6]{0,1,2:T(4,128)S(1)}, s32[8,4,6]{0,1,2:T(4,128)}, u32[]{:S(2)}) copy-start(s32[8,4,6]{0,1,2:T(4,128)} %param.7) | copy-start | bytes 2308
  8.2 6.5 %collective-permute-start = (bf16[1,4,128,128]{2,3,1,0:T(8,128)(2,1)S(1)}, bf16[1,4,128,128]{2,3,1,0:T(8,128)(2,1)S(1)}, u32[]{:S(2)}, u32[]{:S(2)}) collective-permute-start(bf16[1,4,128,128]{2,3,1,0:T(8,128)(2,1)S(1)} %get-tuple-element.15), channel_id=1, source_target_pairs={{0,8},{8,16},{16,24},{24,32},{32,40},{40,48},{48,56},{56,64},{64,7... | collective-permute-start | bytes 393224 | tf_op jit(solution)/shard_map/ppermute | solution.py:113
  12.8 6.3 %collective-permute-start.1 = (bf16[1,4,128,128]{2,3,1,0:T(8,128)(2,1)S(1)}, bf16[1,4,128,128]{2,3,1,0:T(8,128)(2,1)S(1)}, u32[]{:S(2)}, u32[]{:S(2)}) collective-permute-start(bf16[1,4,128,128]{2,3,1,0:T(8,128)(2,1)S(1)} %get-tuple-element.16), channel_id=1, source_target_pairs={{8,0},{16,8},{24,16},{32,24},{40,32},{48,40},{56,48},{64,56},{72,6... | collective-permute-start | bytes 393224 | tf_op jit(solution)/shard_map/ppermute | solution.py:115
  19.2 8.5 %collective-permute-start.2 = (bf16[10,1,128,128]{2,3,1,0:T(8,128)(2,1)S(1)}, bf16[10,1,128,128]{2,3,1,0:T(8,128)(2,1)S(1)}, u32[]{:S(2)}, u32[]{:S(2)}) collective-permute-start(bf16[10,1,128,128]{2,3,1,0:T(8,128)(2,1)S(1)} %get-tuple-element.9), channel_id=1, source_target_pairs={{0,1},{1,2},{2,3},{3,4},{4,5},{5,6},{6,7},{8,9},{9,10},{10,11},{11... | collective-permute-start | bytes 983048 | tf_op jit(solution)/shard_map/ppermute | solution.py:113
  22.8 9.1 %collective-permute-start.3 = (bf16[10,1,128,128]{2,3,1,0:T(8,128)(2,1)S(1)}, bf16[10,1,128,128]{2,3,1,0:T(8,128)(2,1)}, u32[]{:S(2)}, u32[]{:S(2)}) collective-permute-start(bf16[10,1,128,128]{2,3,1,0:T(8,128)(2,1)S(1)} %get-tuple-element.10), channel_id=1, source_target_pairs={{1,0},{2,1},{3,2},{4,3},{5,4},{6,5},{7,6},{9,8},{10,9},{11,10},{12... | collective-permute-start | bytes 983048 | tf_op jit(solution)/shard_map/ppermute | solution.py:115
  27.7 0.7 copy-start.1
  106.3 4.3 %collective-permute-start.4 = (bf16[1,4,128,128]{2,3,1,0:T(8,128)(2,1)S(1)}, bf16[1,4,128,128]{2,3,1,0:T(8,128)(2,1)S(1)}, u32[]{:S(2)}, u32[]{:S(2)}) collective-permute-start(bf16[1,4,128,128]{2,3,1,0:T(8,128)(2,1)S(1)} %get-tuple-element.13), channel_id=1, source_target_pairs={{0,8},{8,16},{16,24},{24,32},{32,40},{40,48},{48,56},{56,64},{64,7... | collective-permute-start | bytes 393224 | tf_op jit(solution)/shard_map/ppermute | solution.py:113
  108.5 6.3 %collective-permute-start.5 = (bf16[1,4,128,128]{2,3,1,0:T(8,128)(2,1)S(1)}, bf16[1,4,128,128]{2,3,1,0:T(8,128)(2,1)S(1)}, u32[]{:S(2)}, u32[]{:S(2)}) collective-permute-start(bf16[1,4,128,128]{2,3,1,0:T(8,128)(2,1)S(1)} %get-tuple-element.14), channel_id=1, source_target_pairs={{8,0},{16,8},{24,16},{32,24},{40,32},{48,40},{56,48},{64,56},{72,6... | collective-permute-start | bytes 393224 | tf_op jit(solution)/shard_map/ppermute | solution.py:115
  114.8 7.5 %collective-permute-start.6 = (bf16[10,1,128,128]{2,3,1,0:T(8,128)(2,1)S(1)}, bf16[10,1,128,128]{2,3,1,0:T(8,128)(2,1)S(1)}, u32[]{:S(2)}, u32[]{:S(2)}) collective-permute-start(bf16[10,1,128,128]{2,3,1,0:T(8,128)(2,1)S(1)} %get-tuple-element.7), channel_id=1, source_target_pairs={{0,1},{1,2},{2,3},{3,4},{4,5},{5,6},{6,7},{8,9},{9,10},{10,11},{11... | collective-permute-start | bytes 983048 | tf_op jit(solution)/shard_map/ppermute | solution.py:113
  117.1 9.3 %collective-permute-start.7 = (bf16[10,1,128,128]{2,3,1,0:T(8,128)(2,1)S(1)}, bf16[10,1,128,128]{2,3,1,0:T(8,128)(2,1)S(1)}, u32[]{:S(2)}, u32[]{:S(2)}) collective-permute-start(bf16[10,1,128,128]{2,3,1,0:T(8,128)(2,1)S(1)} %get-tuple-element.8), channel_id=1, source_target_pairs={{1,0},{2,1},{3,2},{4,3},{5,4},{6,5},{7,6},{9,8},{10,9},{11,10},{12... | collective-permute-start | bytes 983048 | tf_op jit(solution)/shard_map/ppermute | solution.py:115
  141.9 66.8 %collective-permute-start.8 = (bf16[1,4,128,128]{2,3,1,0:T(8,128)(2,1)}, bf16[1,4,128,128]{2,3,1,0:T(8,128)(2,1)S(1)}, u32[]{:S(2)}, u32[]{:S(2)}) collective-permute-start(bf16[1,4,128,128]{2,3,1,0:T(8,128)(2,1)} %get-tuple-element.11), channel_id=1, source_target_pairs={{0,8},{8,16},{16,24},{24,32},{32,40},{40,48},{48,56},{56,64},{64,7... | collective-permute-start | bytes 393224 | tf_op jit(solution)/shard_map/ppermute | solution.py:113
  146.6 62.2 %collective-permute-start.9 = (bf16[1,4,128,128]{2,3,1,0:T(8,128)(2,1)}, bf16[1,4,128,128]{2,3,1,0:T(8,128)(2,1)S(1)}, u32[]{:S(2)}, u32[]{:S(2)}) collective-permute-start(bf16[1,4,128,128]{2,3,1,0:T(8,128)(2,1)} %get-tuple-element.12), channel_id=1, source_target_pairs={{8,0},{16,8},{24,16},{32,24},{40,32},{48,40},{56,48},{64,56},{72,6... | collective-permute-start | bytes 393224 | tf_op jit(solution)/shard_map/ppermute | solution.py:115
  208.8 8.9 %collective-permute-start.10 = (bf16[10,1,128,128]{2,3,1,0:T(8,128)(2,1)S(1)}, bf16[10,1,128,128]{2,3,1,0:T(8,128)(2,1)S(1)}, u32[]{:S(2)}, u32[]{:S(2)}) collective-permute-start(bf16[10,1,128,128]{2,3,1,0:T(8,128)(2,1)S(1)} %get-tuple-element.5), channel_id=1, source_target_pairs={{0,1},{1,2},{2,3},{3,4},{4,5},{5,6},{6,7},{8,9},{9,10},{10,11},{11... | collective-permute-start | bytes 983048 | tf_op jit(solution)/shard_map/ppermute | solution.py:113
  211.1 10.5 %collective-permute-start.11 = (bf16[10,1,128,128]{2,3,1,0:T(8,128)(2,1)S(1)}, bf16[10,1,128,128]{2,3,1,0:T(8,128)(2,1)S(1)}, u32[]{:S(2)}, u32[]{:S(2)}) collective-permute-start(bf16[10,1,128,128]{2,3,1,0:T(8,128)(2,1)S(1)} %get-tuple-element.6), channel_id=1, source_target_pairs={{1,0},{2,1},{3,2},{4,3},{5,4},{6,5},{7,6},{9,8},{10,9},{11,10},{12... | collective-permute-start | bytes 983048 | tf_op jit(solution)/shard_map/ppermute | solution.py:115

commit v2 on v0

v2 whole, which is shorter than its diff:
```python
import functools

import jax
import jax.numpy as jnp
from jax import lax
from jax.experimental import pallas as pl
from jax.experimental.pallas import tpu as pltpu
from jax.sharding import PartitionSpec as P

NEAR = 8
FAR = 16
STRIP = 16
BX, BY, K, N = 8, 4, 6, 128
MESH = pl.DeviceIdType.MESH
F32, BF16 = jnp.float32, jnp.bfloat16
UP, DOWN, CORNER = 16, 17, 18
COPIES = 22


def where_am_i():
    gx, gy = lax.axis_index("gx"), lax.axis_index("gy")
    return gx, gy, lax.rem(gx, NEAR), (gx // NEAR) * 8 + gy


def near_partner(step):
    gx, gy, near, _ = where_am_i()
    at = lax.rem(near + step, NEAR)
    return at, (gx - near + at, gy)


def far_partner(step):
    _, _, near, far = where_am_i()
    to = lax.rem(far + step, FAR)
    return ((to // 8) * NEAR + near, lax.rem(to, 8))


def beside(dx, dy):
    gx, gy, _, _ = where_am_i()
    return (lax.rem(gx + dx + 16, 16), lax.rem(gy + dy + 8, 8))


def remote(src, dst, send, recv, device):
    return pltpu.make_async_remote_copy(
        src_ref=src, dst_ref=dst, send_sem=send, recv_sem=recv, device_id=device, device_id_type=MESH
    )


def greet():
    barrier = pltpu.get_barrier_semaphore()
    partners = [near_partner(s)[1] for s in range(1, NEAR)] + [far_partner(s) for s in range(1, FAR)]
    partners += [beside(dx, dy) for dx in (-1, 0, 1) for dy in (-1, 0, 1) if dx or dy]
    for device in partners:
        pl.semaphore_signal(barrier, inc=1, device_id=device, device_id_type=MESH)
    return functools.partial(pl.semaphore_wait, barrier, len(partners))


def strip_of(ref, at):
    return ref.at[pl.ds(pl.multiple_of(at * STRIP, STRIP), STRIP)]


class Sum:
    def __init__(self, mine, near_buf, mid, far_buf, done, out, near_sems, far_sems):
        self.mine, self.near_buf, self.mid, self.far_buf = mine, near_buf, mid, far_buf
        self.done, self.out = done, out
        _, _, self.near, self.far = where_am_i()
        self.first, self.second, self.third = [], [], []
        for s in range(1, NEAR):
            at, device = near_partner(s)
            self.first.append(remote(
                strip_of(mine, at), near_buf.at[self.near], near_sems.at[0, s], near_sems.at[1, s], device))
            self.third.append(remote(
                done, strip_of(out, self.near), near_sems.at[2, s], near_sems.at[3, s], device))
        for s in range(1, FAR):
            self.second.append(remote(
                mid, far_buf.at[self.far], far_sems.at[0, s], far_sems.at[1, s], far_partner(s)))

    def begin(self):
        for copy in self.first:
            copy.start()
        self.near_buf[self.near] = strip_of(self.mine, self.near)[...]

    def middle(self):
        for copy in self.first:
            copy.wait_recv()
        part = self.near_buf[0]
        for i in range(1, NEAR):
            part = part + self.near_buf[i]
        self.mid[...] = part
        self.far_buf[self.far] = part
        for copy in self.second:
            copy.start()

    def last(self):
        for copy in self.second:
            copy.wait_recv()
        part = self.far_buf[0]
        for i in range(1, FAR):
            part = part + self.far_buf[i]
        self.done[...] = part
        strip_of(self.out, self.near)[...] = part
        for copy in self.third:
            copy.start()

    def end(self):
        for copy in self.third:
            copy.wait_recv()

    def drain(self):
        for copy in self.first + self.second + self.third:
            copy.wait_send()


class Rim:
    def __init__(self, own, table, send, recv):
        self.own, self.table, self.send, self.recv = own, table, send, recv

    def put(self, p, q, block):
        self.own[p, q] = block
        self.table[p + 1, q + 1] = block

    def copy(self, at, src, dst, device):
        return remote(src, dst, self.send.at[at], self.recv.at[at], device)

    def left(self, p):
        return self.copy(p, self.own.at[p, 0], self.table.at[p + 1, 5], beside(0, -1))

    def right(self, p):
        return self.copy(p + 8, self.own.at[p, 3], self.table.at[p + 1, 0], beside(0, 1))

    def sides(self, p):
        return [self.left(p), self.right(p)]

    def ends(self):
        own, t = self.own, self.table
        inner = pl.ds(1, 4)
        return [
            self.copy(UP, own.at[0], t.at[9, inner], beside(-1, 0)),
            self.copy(DOWN, own.at[7], t.at[0, inner], beside(1, 0)),
            self.copy(CORNER, own.at[0, 0], t.at[9, 5], beside(-1, -1)),
            self.copy(CORNER + 1, own.at[0, 3], t.at[9, 0], beside(-1, 1)),
            self.copy(CORNER + 2, own.at[7, 0], t.at[0, 5], beside(1, -1)),
            self.copy(CORNER + 3, own.at[7, 3], t.at[0, 0], beside(1, 1)),
        ]

    def drain(self):
        @pl.loop(0, BX)
        def _(p):
            for copy in self.sides(p):
                copy.wait_send()

        for copy in self.ends():
            copy.wait_send()


def pieces(x):
    high = x.astype(BF16)
    rest = x - high.astype(F32)
    mid = rest.astype(BF16)
    low = (rest - mid.astype(F32)).astype(BF16)
    return high, mid, low


def contract_rows(a, b):
    return lax.dot_general(a, b, (((0,), (0,)), ((), ())), preferred_element_type=F32)


def pair(left, right, wide, thin_a, thin_b):
    for total in (wide, thin_a, thin_b):
        total[...] = jnp.zeros(total.shape, F32)

    @pl.loop(0, 8)
    def _(c):
        lh, lm, ll = pieces(left[pl.ds(c * 4, 4)].reshape(512, N))
        if right is None:
            rh, rm, rl = lh, lm, ll
        else:
            rh, rm, rl = pieces(right[pl.ds(c * 4, 4)].reshape(512, N))
        big = contract_rows(jnp.concatenate([lh, lm], 1), jnp.concatenate([rh, rm], 1))
        small = contract_rows(lh, rl)
        other = None if right is None else contract_rows(ll, rh)
        wide[...] += big
        thin_a[...] += small
        if other is not None:
            thin_b[...] += other

    small = thin_a[...]
    small = small + (small.T if right is None else thin_b[...])
    return wide[:N, :N] + (wide[:N, N:] + wide[N:, :N] + (wide[N:, N:] + small))


def factor_block(b, work, inverse):
    at = 8 * b
    lane = lax.broadcasted_iota(jnp.int32, (8, N), 1)
    rows = [work[pl.ds(at + c, 8, stride=0), :] for c in range(8)]
    a = [[jnp.broadcast_to(rows[i][:, at + k : at + k + 1], (8, N)) for k in range(i + 1)] for i in range(8)]
    rows = [jnp.where((lane >= at) & (lane < at + 8), jnp.where(lane == at + c, 1.0, 0.0), rows[c]) for c in range(8)]
    out = []
    for t in range(8):
        r = lax.rsqrt(a[t][t])
        r = r * (1.5 - (0.5 * a[t][t]) * (r * r))
        new = rows[t] * r
        out.append(new)
        for i in range(t + 1, 8):
            a[i][t] = a[i][t] * r
        for i in range(t + 1, 8):
            for k in range(t + 1, i + 1):
                a[i][k] = a[i][k] - a[i][t] * a[k][t]
            rows[i] = rows[i] - a[i][t] * new
    sub = lax.broadcasted_iota(jnp.int32, (8, N), 0)
    block = out[0]
    for i in range(1, 8):
        block = jnp.where(sub == i, out[i], block)
    inverse[pl.ds(at, 8), :] = jnp.where(lane <= at + sub, block, 0.0)
    if b < 15:
        h, m, l = (x.astype(F32) for x in pieces(block))
        left = [jnp.where(lane >= at + 8, x, 0.0) for x in (h, m, l)]
        hl, ml, ll = left
        lefts = jnp.concatenate([hl, ml, hl, ml, hl, ll], 0).astype(BF16)
        rights = jnp.concatenate([h, h, m, m, l, h], 0).astype(BF16)
        update = contract_rows(lefts, rights)
        below = pl.ds(at + 8, N - at - 8)
        full = lax.broadcasted_iota(jnp.int32, (N - at - 8, N), 1)
        old = work[below, :]
        work[below, :] = jnp.where((full >= at) & (full < at + 8), 0.0, old) - update[at + 8 :]


def times_transposed(x, parts):
    h, m, l = pieces(x)
    bh, bm, bl = parts
    dot = functools.partial(jnp.dot, preferred_element_type=F32)
    deep = jnp.concatenate([h, m], 1)
    big = dot(deep, jnp.concatenate([jnp.concatenate([bh, bh], 0), jnp.concatenate([bm, bm], 0)], 1))
    small = dot(jnp.concatenate([h, l], 1), jnp.concatenate([bl, bh], 0))
    return big[:, :N] + (big[:, N:] + small)


def main_kernel(
    cols, values_hbm, panel_hbm, first_hbm, iterate_hbm, inverse_out, moment_out,
    values, panel, scale, owns, tables, y1, y2, q1, wide, thin_a, thin_b, work, inv1,
    sums_mine, sums_near, sums_mid, sums_far, sums_done, sums_out,
    load_sems, near_sems, far_sems, rim_send, rim_recv,
):
    gx, gy, _, _ = where_am_i()
    rims = [Rim(owns[i], tables[i], rim_send.at[i], rim_recv.at[i]) for i in range(3)]
    sums = [
        Sum(sums_mine.at[i], sums_near.at[i], sums_mid.at[i], sums_far.at[i], sums_done.at[i],
            moment_out if i == 2 else sums_out.at[i], near_sems.at[i], far_sems.at[i])
        for i in range(3)
    ]

    def load(p):
        four = pl.ds(p * 4, 4)
        return [
            pltpu.make_async_copy(values_hbm.at[p], values.at[four], load_sems.at[p]),
            pltpu.make_async_copy(panel_hbm.at[p], panel.at[four], load_sems.at[p + 8]),
        ]

    for p in range(BX):
        for copy in load(p):
            copy.start()
    met = greet()
    met()

    ones = jnp.ones((2 * N, N), BF16)

    @pl.loop(0, BX)
    def _(p):
        for copy in load(p):
            copy.wait()
        for q in range(BY):
            i = p * BY + q
            degree = jnp.zeros((N, N), F32)
            for j in range(3):
                both = jnp.concatenate([values[i, 2 * j], values[i, 2 * j + 1]], 1)
                degree = degree + jnp.dot(both, ones, preferred_element_type=F32)
            s = 1.0 / jnp.sqrt(degree)
            scale[i] = s
            rims[0].put(p, q, (s * panel[i]).astype(BF16))
        for copy in rims[0].sides(p):
            copy.start()

    for copy in rims[0].ends():
        copy.start()

    def block_row(table, p, q, edge):
        i = p * BY + q
        total = jnp.zeros((N, N), F32)
        for j in range(3):
            picked = []
            for k in (2 * j, 2 * j + 1):
                c = cols[p, q, k]
                at_x = jnp.clip((c >> 5) - gx * BX + edge, 0, BX - 1 + 2 * edge)
                at_y = jnp.clip((c & 31) - gy * BY + edge, 0, BY - 1 + 2 * edge)
                picked.append(table[at_x, at_y])
            both = jnp.concatenate([values[i, 2 * j], values[i, 2 * j + 1]], 1)
            total = total + jnp.dot(both, jnp.concatenate(picked, 0), preferred_element_type=F32)
        return scale[i] * total

    def sweep(rim, put, between=()):
        between = list(between) + [lambda: None] * 2

        @pl.loop(1, BX - 1)
        def _(p):
            for q in (1, 2):
                put(p, q, block_row(rim.own, p, q, 0))

        between[0]()

        @pl.loop(0, BX)
        def _(p):
            for copy in rim.sides(p):
                copy.wait_recv()

        for copy in rim.ends():
            copy.wait_recv()

        @pl.loop(1, BX - 1)
        def _(p):
            for q in (0, 3):
                put(p, q, block_row(rim.table, p, q, 1))

        between[1]()

        @pl.loop(0, 2)
        def _(e):
            for q in range(BY):
                put(e * (BX - 1), q, block_row(rim.table, e * (BX - 1), q, 1))

    def put1(p, q, y):
        y1[p * BY + q] = y

    sweep(rims[0], put1)
    sums_mine[0] = pair(y1, None, wide, thin_a, thin_b)
    sums[0].begin()
    sums[0].middle()
    sums[0].last()
    sums[0].end()
    work[...] = sums_out[0] * (1.0 / 524288.0)
    for b in range(16):
        factor_block(b, work, inv1)
    parts = pieces(inv1[...].T)

    def embed(p, q):
        i = p * BY + q
        out = times_transposed(y1[i], parts)
        q1[i] = out
        rims[1].put(p, q, (scale[i] * out).astype(BF16))

    @pl.loop(0, BX)
    def _(p):
        embed(p, 0)
        embed(p, 3)
        for copy in rims[1].sides(p):
            copy.start()

    @pl.loop(0, 2)
    def _(e):
        embed(e * (BX - 1), 1)
        embed(e * (BX - 1), 2)

    for copy in rims[1].ends():
        copy.start()

    @pl.loop(1, BX - 1)
    def _(p):
        embed(p, 1)
        embed(p, 2)

    first_copy = pltpu.make_async_copy(q1, first_hbm, load_sems.at[16])
    first_copy.start()

    def put2(p, q, y):
        i = p * BY + q
        y2[i] = y
        rims[2].put(p, q, (scale[i] * y).astype(BF16))

    sweep(rims[1], put2)

    @pl.loop(0, BX)
    def _(p):
        for copy in rims[2].sides(p):
            copy.start()

    for copy in rims[2].ends():
        copy.start()
    second_copy = pltpu.make_async_copy(y2, iterate_hbm, load_sems.at[17])
    second_copy.start()
    sums_mine[1] = pair(y2, None, wide, thin_a, thin_b)
    sums[1].begin()
    sweep(rims[2], put1, (sums[1].middle, sums[1].last))
    sums_mine[2] = pair(y2, y1, wide, thin_a, thin_b)
    sums[2].begin()
    sums[1].end()
    work[...] = sums_out[1] * (1.0 / 524288.0)
    for b in range(16):
        if b == 5:
            sums[2].middle()
        if b == 11:
            sums[2].last()
        factor_block(b, work, inverse_out)
    sums[2].end()
    first_copy.wait()
    second_copy.wait()
    for s in sums:
        s.drain()
    for rim in rims:
        rim.drain()


def last_kernel(inverse, moment, iterate, embedding, ritz):
    hi = lax.Precision.HIGHEST
    inv_t = inverse[...].T
    parts = pieces(inv_t)
    embedding[...] = times_transposed(iterate[...], parts)

    @pl.when(pl.program_id(0) == 0)
    def _():
        left = jnp.dot(inverse[...], moment[...] * (1.0 / 524288.0), precision=hi, preferred_element_type=F32)
        ritz[...] = jnp.dot(left, inv_t, precision=hi, preferred_element_type=F32)


def on_device(values, columns, panel):
    dma = pltpu.SemaphoreType.DMA
    vmem = pltpu.VMEM
    any_space = pl.BlockSpec(memory_space=pl.ANY)
    in_vmem = pl.BlockSpec(memory_space=pltpu.VMEM)
    square = jax.ShapeDtypeStruct((N, N), F32)
    tall = jax.ShapeDtypeStruct((BX * BY, N, N), F32)
    blocks = (BX * BY, N, N)
    first, iterate, inverse, moment = pl.pallas_call(
        main_kernel,
        out_shape=(tall, tall, square, square),
        in_specs=[pl.BlockSpec(memory_space=pltpu.SMEM), any_space, any_space],
        out_specs=(any_space, any_space, in_vmem, in_vmem),
        scratch_shapes=[
            vmem((BX * BY, K, N, N), BF16), vmem(blocks, F32), vmem(blocks, F32),
            [vmem((BX, BY, N, N), BF16) for _ in range(3)],
            [vmem((BX + 2, BY + 2, N, N), BF16) for _ in range(3)],
            vmem(blocks, F32), vmem(blocks, F32), vmem(blocks, F32),
            vmem((2 * N, 2 * N), F32), vmem((N, N), F32), vmem((N, N), F32), vmem((N, N), F32), vmem((N, N), F32),
            vmem((3, N, N), F32), vmem((3, NEAR, STRIP, N), F32), vmem((3, STRIP, N), F32),
            vmem((3, FAR, STRIP, N), F32), vmem((3, STRIP, N), F32), vmem((3, N, N), F32),
            dma((18,)), dma((3, 4, NEAR)), dma((3, 2, FAR)), dma((3, COPIES)), dma((3, COPIES)),
        ],
        compiler_params=pltpu.CompilerParams(
            collective_id=0, has_side_effects=True, vmem_limit_bytes=48 * 1024 * 1024),
        name="iterate_all",
    )(columns, values, panel)
    rows = BX * BY * N
    embedding, ritz = pl.pallas_call(
        last_kernel,
        grid=(4,),
        out_shape=(jax.ShapeDtypeStruct((rows, N), F32), square),
        in_specs=[
            pl.BlockSpec((N, N), lambda i: (0, 0)), pl.BlockSpec((N, N), lambda i: (0, 0)),
            pl.BlockSpec((rows // 4, N), lambda i: (i, 0)),
        ],
        out_specs=(pl.BlockSpec((rows // 4, N), lambda i: (i, 0)), pl.BlockSpec((N, N), lambda i: (0, 0))),
        name="embed_last",
    )(inverse, moment, iterate.reshape(rows, N))
    return first.reshape(panel.shape), embedding.reshape(panel.shape), ritz


def solution(mesh):
    in_specs = (P("gx", "gy", None, None, None), P("gx", "gy", None), P("gx", "gy", None, None))
    out_specs = (P("gx", "gy", None, None), P("gx", "gy", None, None), P())
    return jax.shard_map(
        on_device, mesh=mesh, in_specs=in_specs, out_specs=out_specs, check_vma=False
    )
```

time: 505 us -> 104 us (0.21); the launches traced: 498 us -> 104 us
  waiting for transfers between devices: 325 us -> 0 us
  Pallas kernels: 0 us -> 98.5 us
  other arithmetic: 58.6 us -> 0 us
  matrix products: 38 us -> 0 us
  starting transfers between devices: 30.6 us -> 0 us
  local copies, waits for them, and re-layouts: 30.9 us -> 4.69 us
  between operations: 14.8 us -> 0.65 us
    psum x2 -> x0, waiting for transfers between devices: 292 us -> none  [the longest x1 148 us: on_device(): gram_sum = lax.psum(local_pair(iterate, iterate), ('gx', 'gy'))]
    pallas_call x0 -> x2, Pallas kernels: none -> 98.5 us  [the longest x1 93.3 us: on_device(): pl.pallas_call(main_kernel, out_shape=(tall, tall, square, square), in_sp...]
    another operation x10 -> x0, other arithmetic: 45.7 us -> none  [the longest x6 24.8 us: lower_inverse(): factor = jnp.linalg.cholesky(gram)]
    dot_general x10 -> x0, matrix products: 37.4 us -> none  [the longest x3 19.2 us: apply_rows(): jnp.einsum('abkij,abkjc->abic', values, picked, preferred_element_type=jn...]
    ppermute x12 -> x0, waiting for transfers between devices: 33 us -> none  [the longest x6 24.6 us: padded_2(): lax.ppermute(head, axis, [((i + 1) % count, i) for i in range(ends)])]
    ppermute x12 -> x0, starting transfers between devices: 30.4 us -> none  [the longest x6 20.3 us: padded_2(): lax.ppermute(tail, axis, [(i, (i + 1) % count) for i in range(ends)])]
    gather x3 -> x0, local copies, waits for them, and re-layouts: 26 us -> none  [apply_rows(): picked = table[flat_index]]
  transfers between devices with their start and end apart: 14 -> 0, of which waited for: 11 -> 0; matrix products, arithmetic and copies ran while one was open for 1% -> 0% of each run, Pallas kernels for 0% -> 0%
where the time goes in v2:
time: 104 us
  Pallas kernels  98.5 us (95%)
  local copies, waits for them, and re-layouts  4.69 us (5%)
    pallas_call x1, Pallas kernels, on_device(): pl.pallas_call(main_kernel, out_shape=(tall, tall, square, square), in_sp...  93.3 us
    pallas_call x1, Pallas kernels, on_device(): pl.pallas_call(last_kernel, grid=(4,), out_shape=(jax.ShapeDtypeStruct((r...  5.23 us
    unnamed x8, local copies, waits for them, and re-layouts  4.69 us

profile of v2, /device:TPU:1, one launch (start us, length us, event | category | flops | bytes accessed | tf_op | source)
XLA Modules:
  0.0 103.8 jit_solution(3458905273304253256)
XLA Ops:
  0.6 0.8 copy.6.cols
  1.4 93.3 %iterate_all.1 = (f32[32,128,128]{2,1,0:T(8,128)S(1)}, f32[32,128,128]{2,1,0:T(8,128)S(1)}, f32[128,128]{1,0:T(8,128)S(1)}, f32[128,128]{1,0:T(8,128)S(1)}) custom-call(s32[8,4,6]{2,1,0:T(4,128)S(1)} %copy.6.cols, bf16[8,4,6,128,128]{4,3,2,1,0:T(8,128)(2,1)} %values_hbm.1, f32[8,4,128,128]{3,2,1,0:T(8,128)} %panel_hbm.1), custom_call_target="tpu_custom_call" | custom-call | tf_op jit(solution)/shard_map/iterate_all/pallas_call | solution.py:430
  94.7 0.0 copy-start
  94.7 1.3 %copy-done = f32[32,128,128]{2,1,0:T(8,128)} copy-done((f32[32,128,128]{2,1,0:T(8,128)}, f32[32,128,128]{2,1,0:T(8,128)S(1)}, u32[]{:S(2)}) %copy-start) | copy-done | bytes 2097176
  96.0 0.0 copy-start.1
  96.0 0.6 copy-done.1
  96.7 0.0 copy-start.2
  96.7 0.6 copy-done.2
  97.3 5.2 %embed_last.1 = (f32[4096,128]{1,0:T(8,128)}, f32[128,128]{1,0:T(8,128)}) custom-call(f32[128,128]{1,0:T(8,128)} %copy-done.1, f32[128,128]{1,0:T(8,128)} %copy-done.2, f32[4096,128]{1,0:T(8,128)} %bitcast.4), custom_call_target="tpu_custom_call" | custom-call | tf_op jit(solution)/shard_map/embed_last/pallas_call | solution.py:450
  102.5 1.3 %copy.8 = f32[8,4,128,128]{3,2,1,0:T(8,128)} copy(f32[8,4,128,128]{3,2,1,0:T(8,128)S(1)} %bitcast.3) | data formatting | bytes 4194304
Async XLA Ops:
  94.7 1.3 %copy-start = (f32[32,128,128]{2,1,0:T(8,128)}, f32[32,128,128]{2,1,0:T(8,128)S(1)}, u32[]{:S(2)}) copy-start(f32[32,128,128]{2,1,0:T(8,128)S(1)} %get-tuple-element.12) | copy-start | bytes 6291460
  96.0 0.6 copy-start.1
  96.7 0.6 copy-start.2

commit v3 on v2

--- a/solution.py
+++ b/solution.py
@@ -235,13 +235,13 @@
 
 
 def main_kernel(
-    cols, values_hbm, panel_hbm, first_hbm, iterate_hbm, inverse_out, moment_out,
-    values, panel, scale, owns, tables, y1, y2, q1, wide, thin_a, thin_b, work, inv1,
+    cols, values_hbm, panel_hbm, q1, y2, inverse_out, moment_out,
+    values, panel, scale, owns, tables, scaled, halo, y1, wide, thin_a, thin_b, work, inv1,
     sums_mine, sums_near, sums_mid, sums_far, sums_done, sums_out,
     load_sems, near_sems, far_sems, rim_send, rim_recv,
 ):
     gx, gy, _, _ = where_am_i()
-    rims = [Rim(owns[i], tables[i], rim_send.at[i], rim_recv.at[i]) for i in range(3)]
+    rims = {i: Rim(owns[i // 2], tables[i], rim_send.at[i], rim_recv.at[i]) for i in (0, 2)}
     sums = [
         Sum(sums_mine.at[i], sums_near.at[i], sums_mid.at[i], sums_far.at[i], sums_done.at[i],
             moment_out if i == 2 else sums_out.at[i], near_sems.at[i], far_sems.at[i])
@@ -259,7 +259,6 @@
         for copy in load(p):
             copy.start()
     met = greet()
-    met()
 
     ones = jnp.ones((2 * N, N), BF16)
 
@@ -276,6 +275,11 @@
             s = 1.0 / jnp.sqrt(degree)
             scale[i] = s
             rims[0].put(p, q, (s * panel[i]).astype(BF16))
+
+    met()
+
+    @pl.loop(0, BX)
+    def _(p):
         for copy in rims[0].sides(p):
             copy.start()
 
@@ -288,7 +292,7 @@
         for j in range(3):
             picked = []
             for k in (2 * j, 2 * j + 1):
-                c = cols[p, q, k]
+                c = cols[k, q, p]
                 at_x = jnp.clip((c >> 5) - gx * BX + edge, 0, BX - 1 + 2 * edge)
                 at_y = jnp.clip((c & 31) - gy * BY + edge, 0, BY - 1 + 2 * edge)
                 picked.append(table[at_x, at_y])
@@ -327,96 +331,140 @@
                 put(e * (BX - 1), q, block_row(rim.table, e * (BX - 1), q, 1))
 
     def put1(p, q, y):
+        i = p * BY + q
+        y1[i] = y
+        scaled[p, q] = scale[i] * y
+
+    def put3(p, q, y):
         y1[p * BY + q] = y
 
     sweep(rims[0], put1)
+    wide_rim = Rim(scaled, halo, rim_send.at[1], rim_recv.at[1])
+
+    def send_sides(rim, low, high):
+        @pl.loop(low, high)
+        def _(p):
+            for copy in rim.sides(p):
+                copy.start()
+
+    def send_ends(rim):
+        for copy in rim.ends():
+            copy.start()
+
+    def all_here(rim):
+        @pl.loop(0, BX)
+        def _(p):
+            for copy in rim.sides(p):
+                copy.wait_recv()
+
+        for copy in rim.ends():
+            copy.wait_recv()
+
+    send_sides(wide_rim, 0, 4)
     sums_mine[0] = pair(y1, None, wide, thin_a, thin_b)
     sums[0].begin()
     sums[0].middle()
     sums[0].last()
+    send_ends(wide_rim)
+    send_sides(wide_rim, 4, BX)
     sums[0].end()
     work[...] = sums_out[0] * (1.0 / 524288.0)
     for b in range(16):
         factor_block(b, work, inv1)
     parts = pieces(inv1[...].T)
 
-    def embed(p, q):
-        i = p * BY + q
-        out = times_transposed(y1[i], parts)
-        q1[i] = out
-        rims[1].put(p, q, (scale[i] * out).astype(BF16))
+    table = tables[1]
 
     @pl.loop(0, BX)
     def _(p):
-        embed(p, 0)
-        embed(p, 3)
-        for copy in rims[1].sides(p):
-            copy.start()
+        four = pl.ds(p * BY, BY)
+        out = times_transposed(y1[four].reshape(BY * N, N), parts).reshape(BY, N, N)
+        q1[four] = out
+        table[p + 1, pl.ds(1, BY)] = (scale[four] * out).astype(BF16)
+
+    all_here(wide_rim)
+
+    @pl.loop(0, BX)
+    def _(p):
+        both = jnp.concatenate([halo[p + 1, 0], halo[p + 1, 5]], 0)
+        out = times_transposed(both, parts).astype(BF16)
+        table[p + 1, 0] = out[:N]
+        table[p + 1, 5] = out[N:]
 
     @pl.loop(0, 2)
     def _(e):
-        embed(e * (BX - 1), 1)
-        embed(e * (BX - 1), 2)
-
-    for copy in rims[1].ends():
-        copy.start()
+        out = times_transposed(halo[e * (BX + 1)].reshape((BY + 2) * N, N), parts)
+        table[e * (BX + 1)] = out.astype(BF16).reshape(BY + 2, N, N)
+
+    def put2(p, q):
+        i = p * BY + q
+        y = block_row(table, p, q, 1)
+        y2[i] = y
+        rims[2].put(p, q, (scale[i] * y).astype(BF16))
+
+    @pl.loop(0, BX)
+    def _(p):
+        put2(p, 0)
+        put2(p, 3)
+        for copy in rims[2].sides(p):
+            copy.start()
+
+    @pl.loop(0, 2)
+    def _(e):
+        put2(e * (BX - 1), 1)
+        put2(e * (BX - 1), 2)
+
+    send_ends(rims[2])
 
     @pl.loop(1, BX - 1)
     def _(p):
-        embed(p, 1)
-        embed(p, 2)
-
-    first_copy = pltpu.make_async_copy(q1, first_hbm, load_sems.at[16])
-    first_copy.start()
-
-    def put2(p, q, y):
-        i = p * BY + q
-        y2[i] = y
-        rims[2].put(p, q, (scale[i] * y).astype(BF16))
-
-    sweep(rims[1], put2)
-
-    @pl.loop(0, BX)
-    def _(p):
-        for copy in rims[2].sides(p):
-            copy.start()
-
-    for copy in rims[2].ends():
-        copy.start()
-    second_copy = pltpu.make_async_copy(y2, iterate_hbm, load_sems.at[17])
-    second_copy.start()
+        put2(p, 1)
+        put2(p, 2)
+
     sums_mine[1] = pair(y2, None, wide, thin_a, thin_b)
     sums[1].begin()
-    sweep(rims[2], put1, (sums[1].middle, sums[1].last))
+    sweep(rims[2], put3, (sums[1].middle, sums[1].last))
     sums_mine[2] = pair(y2, y1, wide, thin_a, thin_b)
     sums[2].begin()
     sums[1].end()
     work[...] = sums_out[1] * (1.0 / 524288.0)
     for b in range(16):
-        if b == 5:
+        if b == 11:
             sums[2].middle()
-        if b == 11:
-            sums[2].last()
         factor_block(b, work, inverse_out)
+    sums[2].last()
     sums[2].end()
-    first_copy.wait()
-    second_copy.wait()
     for s in sums:
         s.drain()
-    for rim in rims:
+    for rim in (rims[0], wide_rim, rims[2]):
         rim.drain()
 
 
-def last_kernel(inverse, moment, iterate, embedding, ritz):
+def last_kernel(inverse, moment, first, iterate, first_out, embedding_out, ritz, embedding, sems):
+    first_copy = pltpu.make_async_copy(first, first_out, sems.at[8])
+    first_copy.start()
     hi = lax.Precision.HIGHEST
     inv_t = inverse[...].T
     parts = pieces(inv_t)
-    embedding[...] = times_transposed(iterate[...], parts)
-
-    @pl.when(pl.program_id(0) == 0)
-    def _():
-        left = jnp.dot(inverse[...], moment[...] * (1.0 / 524288.0), precision=hi, preferred_element_type=F32)
-        ritz[...] = jnp.dot(left, inv_t, precision=hi, preferred_element_type=F32)
+
+    def part(c):
+        four = pl.ds(c * 4, 4)
+        return pltpu.make_async_copy(embedding.at[four], embedding_out.at[four], sems.at[c])
+
+    @pl.loop(0, 8)
+    def _(c):
+        four = pl.ds(c * 4, 4)
+        embedding[four] = times_transposed(iterate[four].reshape(4 * N, N), parts).reshape(4, N, N)
+        part(c).start()
+
+    left = jnp.dot(inverse[...], moment[...] * (1.0 / 524288.0), precision=hi, preferred_element_type=F32)
+    ritz[...] = jnp.dot(left, inv_t, precision=hi, preferred_element_type=F32)
+
+    @pl.loop(0, 8)
+    def _(c):
+        part(c).wait()
+
+    first_copy.wait()
 
 
 def on_device(values, columns, panel):
@@ -431,33 +479,30 @@
         main_kernel,
         out_shape=(tall, tall, square, square),
         in_specs=[pl.BlockSpec(memory_space=pltpu.SMEM), any_space, any_space],
-        out_specs=(any_space, any_space, in_vmem, in_vmem),
+        out_specs=(in_vmem,) * 4,
         scratch_shapes=[
             vmem((BX * BY, K, N, N), BF16), vmem(blocks, F32), vmem(blocks, F32),
-            [vmem((BX, BY, N, N), BF16) for _ in range(3)],
+            [vmem((BX, BY, N, N), BF16) for _ in range(2)],
             [vmem((BX + 2, BY + 2, N, N), BF16) for _ in range(3)],
-            vmem(blocks, F32), vmem(blocks, F32), vmem(blocks, F32),
+            vmem((BX, BY, N, N), F32), vmem((BX + 2, BY + 2, N, N), F32), vmem(blocks, F32),
             vmem((2 * N, 2 * N), F32), vmem((N, N), F32), vmem((N, N), F32), vmem((N, N), F32), vmem((N, N), F32),
             vmem((3, N, N), F32), vmem((3, NEAR, STRIP, N), F32), vmem((3, STRIP, N), F32),
             vmem((3, FAR, STRIP, N), F32), vmem((3, STRIP, N), F32), vmem((3, N, N), F32),
-            dma((18,)), dma((3, 4, NEAR)), dma((3, 2, FAR)), dma((3, COPIES)), dma((3, COPIES)),
+            dma((16,)), dma((3, 4, NEAR)), dma((3, 2, FAR)), dma((3, COPIES)), dma((3, COPIES)),
         ],
         compiler_params=pltpu.CompilerParams(
             collective_id=0, has_side_effects=True, vmem_limit_bytes=48 * 1024 * 1024),
         name="iterate_all",
-    )(columns, values, panel)
-    rows = BX * BY * N
-    embedding, ritz = pl.pallas_call(
+    )(columns.transpose(2, 1, 0), values, panel)
+    first, embedding, ritz = pl.pallas_call(
         last_kernel,
-        grid=(4,),
-        out_shape=(jax.ShapeDtypeStruct((rows, N), F32), square),
-        in_specs=[
-            pl.BlockSpec((N, N), lambda i: (0, 0)), pl.BlockSpec((N, N), lambda i: (0, 0)),
-            pl.BlockSpec((rows // 4, N), lambda i: (i, 0)),
-        ],
-        out_specs=(pl.BlockSpec((rows // 4, N), lambda i: (i, 0)), pl.BlockSpec((N, N), lambda i: (0, 0))),
+        out_shape=(tall, tall, square),
+        in_specs=[in_vmem] * 4,
+        out_specs=(any_space, any_space, in_vmem),
+        scratch_shapes=[vmem(blocks, F32), dma((9,))],
+        compiler_params=pltpu.CompilerParams(vmem_limit_bytes=16 * 1024 * 1024),
         name="embed_last",
-    )(inverse, moment, iterate.reshape(rows, N))
+    )(inverse, moment, first, iterate)
     return first.reshape(panel.shape), embedding.reshape(panel.shape), ritz
 
 

time: 104 us -> 94.7 us (0.911)
  Pallas kernels: 98.5 us -> 93.2 us
  local copies, waits for them, and re-layouts: 4.69 us -> 0.7 us
    pallas_call x1, Pallas kernels: 93.3 us -> 89.1 us  [on_device(): pl.pallas_call(main_kernel, out_shape=(tall, tall, square, square), in_sp...]
    unnamed x8 -> x2, local copies, waits for them, and re-layouts: 4.69 us -> 0.7 us
    pallas_call x1, Pallas kernels: 5.23 us -> 4.08 us  [on_device(): pl.pallas_call(last_kernel, out_shape=(tall, tall, square), in_specs=[in_...]
where the time goes in v3:
time: 94.7 us; the launch traced here: 94.5 us
  Pallas kernels  93.2 us (98%)
    pallas_call x1, Pallas kernels, on_device(): pl.pallas_call(main_kernel, out_shape=(tall, tall, square, square), in_sp...  89.1 us
    pallas_call x1, Pallas kernels, on_device(): pl.pallas_call(last_kernel, out_shape=(tall, tall, square), in_specs=[in_...  4.08 us

profile of v3, /device:TPU:1, one launch (start us, length us, event | category | flops | bytes accessed | tf_op | source)
XLA Modules:
  0.0 94.5 jit_solution(12257836287698306044)
XLA Ops:
  0.6 0.0 copy-start
  0.6 0.7 copy-done
  1.3 89.1 %iterate_all.1 = (f32[32,128,128]{2,1,0:T(8,128)S(1)}, f32[32,128,128]{2,1,0:T(8,128)S(1)}, f32[128,128]{1,0:T(8,128)S(1)}, f32[128,128]{1,0:T(8,128)S(1)}) custom-call(s32[6,4,8]{2,1,0:T(4,128)S(1)} %bitcast.3, bf16[8,4,6,128,128]{4,3,2,1,0:T(8,128)(2,1)} %values_hbm.1, f32[8,4,128,128]{3,2,1,0:T(8,128)} %panel_hbm.1), custom_call_target="tpu_custom_call" | custom-call | tf_op jit(solution)/shard_map/iterate_all/pallas_call | solution.py:478
  90.4 4.1 %embed_last.1 = (f32[32,128,128]{2,1,0:T(8,128)}, f32[32,128,128]{2,1,0:T(8,128)}, f32[128,128]{1,0:T(8,128)}) custom-call(f32[128,128]{1,0:T(8,128)S(1)} %get-tuple-element.10.inverse, f32[128,128]{1,0:T(8,128)S(1)} %get-tuple-element.11.moment, f32[32,128,128]{2,1,0:T(8,128)S(1)} %get-tuple-element.12.first, f32[32,128,128]{2,1,0:T(8,128)S(1)} %get-tuple-element.13.iterate), custom_call_target="tpu_custom_call" | custom-call | tf_op jit(solution)/shard_map/embed_last/pallas_call | solution.py:497
Async XLA Ops:
  0.6 0.7 copy-start
